TPU v7x, 256 devices: a whole 4x4x8 slice. The times are simulated.
256 devices in a mesh: seq: 64 (over z, y, core), tp: 4 (over x).
Axes of the slice: x: 4, y: 4, z: 8, core: 2. Of those that a mesh axis runs over, the one named last changes fastest.
Arguments:
- tokens: bfloat16 [128, 1536], replicated, may hold values from -6 to 6
- attn_gain: float32 [1536], replicated, may hold values from 0.25 to 1.75
- qkv_weight: bfloat16 [1536, 2560], P(None, 'tp'), may hold values from -0.15625 to 0.15625
- out_weight: bfloat16 [1536, 1536], P(None, 'tp'), may hold values from -0.15625 to 0.15625
- moe_gain: float32 [1536], P('tp'), may hold values from 0.25 to 1.75
- router_weight: bfloat16 [1536, 40], P('tp'), may hold values from -0.3125 to 0.3125
- expert_gate: bfloat16 [40, 1536, 512], P(None, 'tp', 'seq'), may hold values from -0.15625 to 0.15625
- expert_up: bfloat16 [40, 1536, 512], P(None, 'tp', 'seq'), may hold values from -0.15625 to 0.15625
- expert_down: bfloat16 [40, 512, 1536], P(None, 'seq', 'tp'), may hold values from -0.375 to 0.375
- cache_keys: bfloat16 [32, 2048, 512], P(None, 'seq', 'tp'), may hold values from -240 to 240, as said below
- cache_values: bfloat16 [32, 2048, 512], P(None, 'seq', 'tp'), may hold values from -8 to 8
- lengths: int32 [32], replicated, may hold values from 1 to 32768, as said below
- routes: int32 [128, 8], replicated, may hold values from 0 to 39, all different within a row
Outputs:
- layer_out: bfloat16 [128, 1536], P(None, 'tp')
Inputs may be any that keep to these rules, and one draw needn't show every extreme that they name: `lengths`: one request has exactly 32768 cached positions. `cache_keys`: cached keys are already rotated.
All inputs are finite; a program needn't handle non-finite values.
Results may differ from a plain program's by a relative error of at most 0.014.
Values may be sent and summed in bfloat16 or wider, within the bound.
No kernel may reach another device: no remote copies, remote signals or barrier semaphores. Data moves between devices by JAX's collectives and lax.ppermute only.
A program may use at most 128 MiB of HBM per device.

v0:
```python
import jax
import jax.numpy as jnp
from jax import lax
from jax.sharding import PartitionSpec as P

D = 1536
HEAD = 64
EXPERTS = 40
SINK = 4
NEW = 4
GROUP = 3
EPSILON = 1e-06
ROPE_BASE = 10000.0
FLOOR_SCORE = -1e30


def joined(shard, axis, combine):
    everything = jax.tree.map(lambda part: lax.all_gather(part, axis), shard)
    initial = jax.tree.map(lambda part: part[0], everything)

    def lap(k, so_far):
        return combine(so_far, jax.tree.map(lambda part: part[k], everything))

    return lax.fori_loop(1, lax.axis_size(axis), lap, initial)


def rms_scale(values, gain):
    return values * lax.rsqrt(jnp.mean(values * values, axis=-1, keepdims=True) + EPSILON) * gain


def rotate(values, places):
    half_dim = values.shape[-1] // 2
    freqs = jnp.exp(-jnp.log(ROPE_BASE) * jnp.arange(half_dim, dtype=jnp.float32) / half_dim)
    angles = places.reshape((-1,) + (1,) * (values.ndim - 1)) * freqs
    cosine = jnp.cos(angles)
    sine = jnp.sin(angles)
    first = values[..., :half_dim]
    second = values[..., half_dim:]
    return jnp.concatenate(
        [first * cosine - second * sine, first * sine + second * cosine], axis=-1
    )


def visible(slots, lengths, window):
    lens = lengths[:, None]
    slot_row = slots[None, :]
    live = slot_row < lens
    older = lens - 1 - jnp.mod(lens - 1 - slot_row, window)
    placed = jnp.where(slot_row < SINK, slot_row, older)
    offsets = jnp.arange(NEW, dtype=jnp.int32)
    inside = (slot_row[:, None, :] < SINK) | (
        placed[:, None, :] >= lens[:, :, None] + offsets[None, :, None] - window
    )
    return live[:, None, :] & inside


def combine_parts(earlier, later):
    top_a, mass_a, weighted_a = earlier
    top_b, mass_b, weighted_b = later
    top_both = jnp.maximum(top_a, top_b)
    factor_a = jnp.exp(top_a - top_both)
    factor_b = jnp.exp(top_b - top_both)
    return (
        top_both,
        mass_a * factor_a + mass_b * factor_b,
        weighted_a * factor_a[..., None] + weighted_b * factor_b[..., None],
    )


def on_device(
    tokens,
    attn_gain,
    qkv_weight,
    out_weight,
    moe_gain,
    router_weight,
    expert_gate,
    expert_up,
    expert_down,
    cache_keys,
    cache_values,
    lengths,
    routes,
):
    seq_count = lax.axis_size("seq")
    seq_index = lax.axis_index("seq")
    tp_index = lax.axis_index("tp")
    token_count = tokens.shape[0]
    requests = cache_keys.shape[0]
    slot_count = cache_keys.shape[1]
    window = slot_count * seq_count - SINK
    local_kv = cache_keys.shape[2] // HEAD
    token_full = tokens.astype(jnp.float32)
    normed = rms_scale(token_full, attn_gain).astype(jnp.bfloat16)
    projected = jnp.dot(normed, qkv_weight, preferred_element_type=jnp.float32)
    projected = projected.reshape(token_count, local_kv, GROUP + 2, HEAD)
    places = (
        (lengths[:, None] + jnp.arange(NEW, dtype=jnp.int32)[None, :])
        .reshape(token_count)
        .astype(jnp.float32)
    )
    queries = rotate(projected[:, :, :GROUP], places).astype(jnp.bfloat16)
    new_keys = rotate(projected[:, :, GROUP], places).astype(jnp.bfloat16)
    new_values = projected[:, :, GROUP + 1].astype(jnp.bfloat16)
    query_b = queries.reshape(requests, NEW, local_kv, GROUP, HEAD)
    key_new = new_keys.reshape(requests, NEW, local_kv, HEAD)
    value_new = new_values.reshape(requests, NEW, local_kv, HEAD)
    slots = seq_index * slot_count + jnp.arange(slot_count, dtype=jnp.int32)
    seen = visible(slots, lengths, window)[:, :, None, None, :]
    factor = 1.0 / HEAD**0.5
    key_old = cache_keys.reshape(requests, slot_count, local_kv, HEAD)
    value_old = cache_values.reshape(requests, slot_count, local_kv, HEAD)
    old_scores = (
        jnp.einsum("rtgqd,rsgd->rtgqs", query_b, key_old, preferred_element_type=jnp.float32)
        * factor
    )
    new_scores = (
        jnp.einsum("rtgqd,rugd->rtgqu", query_b, key_new, preferred_element_type=jnp.float32)
        * factor
    )
    causal = jnp.arange(NEW)[:, None] >= jnp.arange(NEW)[None, :]
    own_mask = causal[None, :, None, None, :] & (seq_index == 0)
    old_masked = jnp.where(seen, old_scores, FLOOR_SCORE)
    new_masked = jnp.where(own_mask, new_scores, FLOOR_SCORE)
    top_score = jnp.maximum(jnp.max(old_masked, axis=-1), jnp.max(new_masked, axis=-1))
    old_weights = jnp.where(seen, jnp.exp(old_masked - top_score[..., None]), 0.0)
    new_weights = jnp.where(own_mask, jnp.exp(new_masked - top_score[..., None]), 0.0)
    mass = jnp.sum(old_weights, axis=-1) + jnp.sum(new_weights, axis=-1)
    weighted = jnp.einsum(
        "rtgqs,rsgd->rtgqd", old_weights, value_old.astype(jnp.float32)
    ) + jnp.einsum("rtgqu,rugd->rtgqd", new_weights, value_new.astype(jnp.float32))
    top_score, mass, weighted = joined((top_score, mass, weighted), "seq", combine_parts)
    attended = (weighted / mass[..., None]).reshape(token_count, -1).astype(jnp.bfloat16)
    feature_part = out_weight.shape[1]
    attn_out = jnp.dot(
        lax.all_gather(attended, "tp", axis=1, tiled=True),
        out_weight,
        preferred_element_type=jnp.float32,
    )
    residual = (
        lax.dynamic_slice_in_dim(token_full, tp_index * feature_part, feature_part, 1) + attn_out
    )
    gained = residual * moe_gain
    squares_local = jnp.sum(residual * residual, axis=-1)
    router_f = router_weight.astype(jnp.float32)
    squares_total = lax.psum(squares_local, "tp")
    scale = lax.rsqrt(squares_total / D + EPSILON)
    logits = lax.psum(
        jnp.dot(gained * scale[:, None], router_f, precision=lax.Precision.HIGHEST), "tp"
    )
    moe_in = (gained * scale[:, None]).astype(jnp.bfloat16)
    chosen = jnp.take_along_axis(logits, routes, axis=1)
    gate_prob = jax.nn.softmax(chosen, axis=-1)
    gate_part = jnp.einsum("td,edf->tef", moe_in, expert_gate, preferred_element_type=jnp.float32)
    up_part = jnp.einsum("td,edf->tef", moe_in, expert_up, preferred_element_type=jnp.float32)
    gate_pick = jnp.take_along_axis(gate_part, routes[:, :, None], axis=1)
    up_pick = jnp.take_along_axis(up_part, routes[:, :, None], axis=1)
    gate_sum, up_sum = (
        lax.psum(gate_pick.astype(jnp.bfloat16), "tp").astype(jnp.float32),
        lax.psum(up_pick.astype(jnp.bfloat16), "tp").astype(jnp.float32),
    )
    activated = (jax.nn.silu(gate_sum) * up_sum).astype(jnp.bfloat16)
    scaled = (gate_prob[:, :, None] * activated.astype(jnp.float32)).astype(jnp.bfloat16)
    onehot = (routes[:, :, None] == jnp.arange(EXPERTS, dtype=jnp.int32)[None, None, :]).astype(
        jnp.bfloat16
    )
    spread = jnp.einsum("tke,tkf->tef", onehot, scaled, preferred_element_type=jnp.float32).astype(
        jnp.bfloat16
    )
    moe_part = jnp.einsum("tef,efd->td", spread, expert_down, preferred_element_type=jnp.float32)
    moe_out = lax.psum(moe_part, "seq")
    return (residual + moe_out).astype(jnp.bfloat16)


def solution(mesh):
    in_specs = (
        P(),
        P(),
        P(None, "tp"),
        P(None, "tp"),
        P("tp"),
        P("tp", None),
        P(None, "tp", "seq"),
        P(None, "tp", "seq"),
        P(None, "seq", "tp"),
        P(None, "seq", "tp"),
        P(None, "seq", "tp"),
        P(),
        P(),
    )
    out_specs = P(None, "tp")
    return jax.shard_map(
        on_device, mesh=mesh, in_specs=in_specs, out_specs=out_specs, check_vma=False
    )
```

profile of v0, /device:TPU:2, one launch (start us, length us, event | category | flops | bytes accessed | tf_op | source)
XLA Modules:
  0.0 648.5 jit_solution(3661215171053748610)
XLA Ops:
  9.3 2.0 fusion.11
  13.8 1.2 reshape.397
  16.1 1.5 fusion.59
  21.6 61.3 %all-gather.1 = f32[2048,4,2,3]{1,2,3,0:T(2,128)S(1)} all-gather(f32[32,4,2,3]{1,2,3,0:T(2,128)S(1)} %copy.167), channel_id=3, replica_groups=mesh['seq'=64,'tp'=4] {'seq'}, dimensions={0}, use_global_device_ids=true | all-gather | bytes 199680 | tf_op jit(solution)/shard_map/all_gather | solution.py:18
  82.9 2.7 copy-done.1
  85.6 8.5 %copy.178 = f32[64,32,4,2,3]{1,3,4,2,0:T(2,128)} copy(f32[64,32,4,2,3]{2,3,4,1,0:T(2,128)} %bitcast.82) | data formatting | bytes 393216 | tf_op jit(solution)/shard_map/while | solution.py:24
  94.2 60.6 %all-gather = f32[2048,4,2,3]{1,2,3,0:T(2,128)S(1)} all-gather(f32[32,4,2,3]{1,2,3,0:T(2,128)S(1)} %copy.166), channel_id=2, replica_groups=mesh['seq'=64,'tp'=4] {'seq'}, dimensions={0}, use_global_device_ids=true | all-gather | bytes 199680 | tf_op jit(solution)/shard_map/all_gather | solution.py:18
  154.8 2.7 copy-done.2
  157.6 8.5 %copy.177 = f32[64,32,4,2,3]{1,3,4,2,0:T(2,128)} copy(f32[64,32,4,2,3]{2,3,4,1,0:T(2,128)} %bitcast.83) | data formatting | bytes 393216 | tf_op jit(solution)/shard_map/while | solution.py:24
  168.4 199.7 %while.19 = (s32[]{:T(128)}, f32[32,4,2,3]{0,2,3,1:T(2,128)S(1)}, f32[32,4,2,3]{0,2,3,1:T(2,128)S(1)}, f32[32,4,2,3,64]{4,3,2,1,0:T(4,128)S(1)}, f32[64,32,4,2,3...) while((s32[]{:T(128)}, f32[32,4,2,3]{0,2,3,1:T(2,128)S(1)}, ...), condition=%wide.region_6.7_spmd, body=%wide.region_5.6_spmd.sunk | while | flops 152069 | bytes 1026199 | solution.py:24
  368.9 13.3 %all_gather.21 = bf16[128,1536]{1,0:T(8,128)(2,1)S(1)} all-gather(bf16[128,384]{1,0:T(8,128)(2,1)S(1)} %convert_element_type.75), channel_id=1, replica_groups=mesh['seq'=64,'tp'=4] {'tp'}, dimensions={1}, use_global_device_ids=true | all-gather | bytes 491520 | tf_op jit(solution)/shard_map/all_gather | solution.py:136
  382.2 1.8 multiply_reduce_fusion.1
  384.0 8.0 %psum.35 = f32[128]{0:T(128)S(1)} all-reduce(f32[128]{0:T(128)S(1)} %get-tuple-element.256), channel_id=1, replica_groups=mesh['seq'=64,'tp'=4] {'tp'}, use_global_device_ids=true, to_apply=%region_8.9 | all-reduce | flops 128 | bytes 1024 | tf_op jit(solution)/shard_map/psum | solution.py:146
  393.5 1.8 copy.191
  395.3 10.5 %gather_fusion.2 = bf16[1024,8]{1,0:T(8,128)(2,1)} fusion(bf16[128,40,8]{2,1,0:T(8,128)(2,1)S(1)} %copy.191, s32[1024]{0:T(1024)S(1)} %reshape.431), kind=kCustom, calls=%fused_computation.1.clone | custom fusion | bytes 40960 | tf_op jit(solution)/shard_map/jit(take_along_axis)/gather | solution.py:157
  405.8 1.7 copy.193
  407.5 1.9 fusion.20
  409.4 1.8 copy.186
  411.2 10.5 %gather_fusion.1 = bf16[1024,8]{1,0:T(8,128)(2,1)} fusion(bf16[128,40,8]{2,1,0:T(8,128)(2,1)S(1)} %copy.186, s32[1024]{0:T(1024)S(1)} %reshape.431), kind=kCustom, calls=%fused_computation.clone | custom fusion | bytes 40960 | tf_op jit(solution)/shard_map/jit(take_along_axis)/gather | solution.py:156
  423.9 15.9 %psum.36 = f32[128,40]{0,1:T(8,128)S(1)} all-reduce(f32[128,40]{0,1:T(8,128)S(1)} %fusion.29), channel_id=1, replica_groups=mesh['seq'=64,'tp'=4] {'tp'}, use_global_device_ids=true, to_apply=%region_9.10 | all-reduce | flops 5120 | bytes 40960 | tf_op jit(solution)/shard_map/psum | solution.py:148
  439.8 7.0 %gather_fusion = f32[1024]{0:T(1024)S(1)} fusion(f32[128,40]{0,1:T(8,128)S(1)} %psum.36, s32[1024]{0:T(1024)S(1)} %reshape.411), kind=kCustom, calls=%fused_computation.2 | custom fusion | bytes 16384 | tf_op jit(solution)/shard_map/jit(take_along_axis)/gather | solution.py:152
  447.1 14.5 %all-reduce = (bf16[128,8,8]{0,2,1:T(8,128)(2,1)S(1)}, bf16[128,8,8]{0,2,1:T(8,128)(2,1)S(1)}) all-reduce(bf16[128,8,8]{0,2,1:T(8,128)(2,1)S(1)} %get-tuple-element.247, bf16[128,8,8]{0,2,1:T(8,128)(2,1)S(1)} %get-tuple-element.246), channel_id=1, replica_groups=mesh['seq'=64,'tp'=4] {'tp'}, use_global_device_ids=true, to_apply=%region_13.15 | all-reduce | flops 16384 | bytes 65536 | tf_op jit(solution)/shard_map/psum | solution.py:160
  463.4 176.7 %all-reduce.3.cloned.1.call-done = f32[128,384]{1,0:T(8,128)} async-done(((f32[128,384]{1,0:T(8,128)}), f32[128,384]{1,0:T(8,128)}) %all-reduce.3.cloned.1.call-update) | async-done | bytes 196624 | tf_op jit(solution)/shard_map/psum | solution.py:171
  640.1 1.6 add_convert_fusion
  (416 shorter events, 216.3 us)
Async XLA Ops:
  6.5 2.7 copy-start
  6.5 4.7 copy-start.15
  6.5 160.7 %all-gather.5.cloned.1.call-start = ((), (), s32[]{:S(2)}) async-start(), calls=%async_computation.1 | async-start | bytes 25559040 | tf_op jit(solution)/shard_map/all_gather | solution.py:18
  9.3 2.8 copy-start.6
  15.1 1.0 copy-start.10
  15.1 1.0 copy-start.11
  16.1 2.0 copy-start.4
  18.1 1.3 copy-start.3
  18.1 2.7 copy-start.5
  19.4 620.7 %all-reduce.3.cloned.1.call-start = ((), (), s32[]{:S(2)}) async-start(), calls=%async_computation | async-start | bytes 393216 | tf_op jit(solution)/shard_map/psum | solution.py:171
  82.9 2.7 copy-start.1
  154.8 2.7 copy-start.2
  157.6 8.6 %copy-start.9 = (s32[128,8]{0,1:T(8,128)S(1)}, s32[128,8]{0,1:T(8,128)}, u32[]{:S(2)}) copy-start(s32[128,8]{0,1:T(8,128)} %param.29) | copy-start | bytes 12292
  368.2 24.4 %copy-start.7 = (bf16[40,384,8]{1,2,0:T(8,128)(2,1)S(1)}, bf16[40,384,8]{1,2,0:T(8,128)(2,1)}, u32[]{:S(2)}) copy-start(bf16[40,384,8]{1,2,0:T(8,128)(2,1)} %param.24) | copy-start | bytes 737284
  368.2 24.4 %copy-start.13 = (f32[384]{0:T(512)S(1)}, f32[384]{0:T(512)}, u32[]{:S(2)}) copy-start(f32[384]{0:T(512)} %param.21) | copy-start | bytes 4612
  392.0 0.5 copy-start.14
  439.8 7.3 %copy-start.12 = (bf16[128,8,8]{0,2,1:T(8,128)(2,1)S(1)}, bf16[128,8,8]{0,2,1:T(8,128)(2,1)}, u32[]{:S(2)}) copy-start(bf16[128,8,8]{0,2,1:T(8,128)(2,1)} %copy.193) | copy-start | bytes 49156
  439.8 7.3 %copy-start.16 = (pred[128,8]{0,1:T(8,128)(4,1)S(1)}, pred[128,8]{0,1:T(8,128)(4,1)}, u32[]{:S(2)}) copy-start(pred[128,8]{0,1:T(8,128)(4,1)} %and_bitcast_fusion) | copy-start | bytes 3076
  446.8 15.6 %copy-start.8 = (bf16[40,8,384]{2,1,0:T(8,128)(2,1)S(1)}, bf16[40,8,384]{2,1,0:T(8,128)(2,1)}, u32[]{:S(2)}) copy-start(bf16[40,8,384]{2,1,0:T(8,128)(2,1)} %param.25) | copy-start | bytes 737284
Sparse Core Ops, SparseCore 0:
  19.5 144.7 all-gather.4
  463.5 176.5 all-reduce.2
where the time goes:
time: 659 us; the launch traced here: 649 us
  waiting for transfers between devices  177 us (27%)
  blocking collectives  174 us (26%)
  local copies, waits for them, and re-layouts  150 us (23%)
  other arithmetic  119 us (18%)
  between operations  13.9 us (2%)
  matrix products  12.6 us (2%)
    psum x1, waiting for transfers between devices, on_device(): moe_out = lax.psum(moe_part, 'seq')  177 us
    all_gather x2, blocking collectives, joined(): everything = jax.tree.map(lambda part: lax.all_gather(part, axis), shard)  122 us
    dynamic_slice x63, local copies, waits for them, and re-layouts, lap(): return combine(so_far, jax.tree.map(lambda part: part[k], everything))  65.7 us
    add x63, other arithmetic, combine_parts(): weighted_a * factor_a[..., None] + weighted_b * factor_b[..., None]  62.8 us
    add x63, other arithmetic, combine_parts(): mass_a * factor_a + mass_b * factor_b  48.3 us
    while x6, local copies, waits for them, and re-layouts, joined(): return lax.fori_loop(1, lax.axis_size(axis), lap, initial)  17.5 us
    psum x1, blocking collectives, on_device(): lax.psum(jnp.dot(gained * scale[:, None], router_f, precision=lax.Precisi...  15.9 us
    psum x1, blocking collectives, on_device(): lax.psum(up_pick.astype(jnp.bfloat16), 'tp').astype(jnp.float32)  14.5 us
  transfers between devices with their start and end apart: 2, of which 1 were waited for; matrix products, arithmetic and copies ran while one was open for 3% of the time, Pallas kernels for 0%

commit v1 on v0

--- a/solution.py
+++ b/solution.py
@@ -168,7 +168,7 @@
         jnp.bfloat16
     )
     moe_part = jnp.einsum("tef,efd->td", spread, expert_down, preferred_element_type=jnp.float32)
-    moe_out = lax.psum(moe_part, "seq")
+    moe_out = jnp.sum(lax.all_gather(moe_part, "seq"), axis=0)
     return (residual + moe_out).astype(jnp.bfloat16)
 
 

time: 659 us -> 553 us (0.84)
  the two profiles are of different devices: /device:TPU:2 before, /device:TPU:1 now
where the time goes in v1:
time: 553 us; the launch traced here: 543 us
  blocking collectives  164 us (30%)
  local copies, waits for them, and re-layouts  133 us (24%)
  other arithmetic  121 us (22%)
  waiting for transfers between devices  99 us (18%)
  between operations  13.9 us (3%)
  matrix products  8.35 us (2%)
    all_gather x2, blocking collectives, joined(): everything = jax.tree.map(lambda part: lax.all_gather(part, axis), shard)  123 us
    all_gather x1, waiting for transfers between devices, on_device(): moe_out = jnp.sum(lax.all_gather(moe_part, 'seq'), axis=0)  98.9 us
    dynamic_slice x63, local copies, waits for them, and re-layouts, lap(): return combine(so_far, jax.tree.map(lambda part: part[k], everything))  65.7 us
    add x63, other arithmetic, combine_parts(): weighted_a * factor_a[..., None] + weighted_b * factor_b[..., None]  61.8 us
    add x63, other arithmetic, combine_parts(): mass_a * factor_a + mass_b * factor_b  48.4 us
    while x6, local copies, waits for them, and re-layouts, joined(): return lax.fori_loop(1, lax.axis_size(axis), lap, initial)  17.7 us
    psum x1, blocking collectives, on_device(): lax.psum(up_pick.astype(jnp.bfloat16), 'tp').astype(jnp.float32)  12.1 us
  transfers between devices with their start and end apart: 2, of which 1 were waited for; matrix products, arithmetic and copies ran while one was open for 4% of the time, Pallas kernels for 0%

profile of v1, /device:TPU:1, one launch (start us, length us, event | category | flops | bytes accessed | tf_op | source)
XLA Modules:
  0.0 542.6 jit_solution(9062822825560332009)
XLA Ops:
  8.1 1.2 multiply_reduce_fusion
  9.3 2.0 fusion.11
  14.0 1.5 fusion.59
  16.0 1.2 fusion.4
  18.5 62.0 %all-gather.1 = f32[2048,4,2,3]{1,2,3,0:T(2,128)S(1)} all-gather(f32[32,4,2,3]{1,2,3,0:T(2,128)S(1)} %copy.167), channel_id=3, replica_groups=mesh['seq'=64,'tp'=4] {'seq'}, dimensions={0}, use_global_device_ids=true | all-gather | bytes 199680 | tf_op jit(solution)/shard_map/all_gather | solution.py:18
  80.5 2.7 copy-done.2
  83.2 8.6 %copy.178 = f32[64,32,4,2,3]{1,3,4,2,0:T(2,128)} copy(f32[64,32,4,2,3]{2,3,4,1,0:T(2,128)} %bitcast.83) | data formatting | bytes 393216 | tf_op jit(solution)/shard_map/while | solution.py:24
  91.9 61.0 %all-gather = f32[2048,4,2,3]{1,2,3,0:T(2,128)S(1)} all-gather(f32[32,4,2,3]{1,2,3,0:T(2,128)S(1)} %copy.166), channel_id=2, replica_groups=mesh['seq'=64,'tp'=4] {'seq'}, dimensions={0}, use_global_device_ids=true | all-gather | bytes 199680 | tf_op jit(solution)/shard_map/all_gather | solution.py:18
  152.9 2.7 copy-done.3
  155.7 8.6 %copy.177 = f32[64,32,4,2,3]{1,3,4,2,0:T(2,128)} copy(f32[64,32,4,2,3]{2,3,4,1,0:T(2,128)} %bitcast.84) | data formatting | bytes 393216 | tf_op jit(solution)/shard_map/while | solution.py:24
  166.1 198.8 %while.19 = (s32[]{:T(128)}, f32[32,4,2,3]{0,2,3,1:T(2,128)S(1)}, f32[32,4,2,3]{0,2,3,1:T(2,128)S(1)}, f32[32,4,2,3,64]{4,3,2,1,0:T(4,128)S(1)}, f32[64,32,4,2,3...) while((s32[]{:T(128)}, f32[32,4,2,3]{0,2,3,1:T(2,128)S(1)}, ...), condition=%wide.region_6.7_spmd, body=%wide.region_5.6_spmd.sunk | while | flops 152069 | bytes 1026199 | solution.py:24
  170.4 1.0 constant_dynamic-slice_fusion.2
  176.7 1.0 constant_dynamic-slice_fusion.2
  183.0 1.0 constant_dynamic-slice_fusion.2
  189.3 1.0 constant_dynamic-slice_fusion.2
  365.7 10.8 %all_gather.27 = bf16[128,1536]{1,0:T(8,128)(2,1)S(1)} all-gather(bf16[128,384]{1,0:T(8,128)(2,1)S(1)} %convert_element_type.75), channel_id=1, replica_groups=mesh['seq'=64,'tp'=4] {'tp'}, dimensions={1}, use_global_device_ids=true | all-gather | bytes 491520 | tf_op jit(solution)/shard_map/all_gather | solution.py:136
  376.9 7.4 %psum.28 = f32[128]{0:T(128)S(1)} all-reduce(f32[128]{0:T(128)S(1)} %get-tuple-element.256), channel_id=1, replica_groups=mesh['seq'=64,'tp'=4] {'tp'}, use_global_device_ids=true, to_apply=%region_8.9 | all-reduce | flops 128 | bytes 1024 | tf_op jit(solution)/shard_map/psum | solution.py:146
  385.3 5.8 %gather_fusion.2 = bf16[1024,8]{1,0:T(8,128)(2,1)S(1)} fusion(bf16[128,40,8]{2,1,0:T(8,128)(2,1)S(1)} %copy.191, s32[1024]{0:T(1024)S(1)} %reshape.432), kind=kCustom, calls=%fused_computation.1.clone | custom fusion | bytes 40960 | tf_op jit(solution)/shard_map/jit(take_along_axis)/gather | solution.py:157
  392.3 5.8 %gather_fusion.1 = bf16[1024,8]{1,0:T(8,128)(2,1)S(1)} fusion(bf16[128,40,8]{2,1,0:T(8,128)(2,1)S(1)} %copy.186, s32[1024]{0:T(1024)S(1)} %reshape.432), kind=kCustom, calls=%fused_computation.clone | custom fusion | bytes 40960 | tf_op jit(solution)/shard_map/jit(take_along_axis)/gather | solution.py:156
  398.7 10.9 %psum.29 = f32[128,40]{0,1:T(8,128)S(1)} all-reduce(f32[128,40]{0,1:T(8,128)S(1)} %fusion.29), channel_id=1, replica_groups=mesh['seq'=64,'tp'=4] {'tp'}, use_global_device_ids=true, to_apply=%region_9.10 | all-reduce | flops 5120 | bytes 40960 | tf_op jit(solution)/shard_map/psum | solution.py:148
  409.7 7.0 %gather_fusion = f32[1024]{0:T(1024)S(1)} fusion(f32[128,40]{0,1:T(8,128)S(1)} %psum.29, s32[1024]{0:T(1024)S(1)} %reshape.411), kind=kCustom, calls=%fused_computation.2 | custom fusion | bytes 16384 | tf_op jit(solution)/shard_map/jit(take_along_axis)/gather | solution.py:152
  416.9 12.1 %all-reduce = (bf16[128,8,8]{0,2,1:T(8,128)(2,1)S(1)}, bf16[128,8,8]{0,2,1:T(8,128)(2,1)S(1)}) all-reduce(bf16[128,8,8]{0,2,1:T(8,128)(2,1)S(1)} %get-tuple-element.247, bf16[128,8,8]{0,2,1:T(8,128)(2,1)S(1)} %get-tuple-element.246), channel_id=1, replica_groups=mesh['seq'=64,'tp'=4] {'tp'}, use_global_device_ids=true, to_apply=%region_13.15 | all-reduce | flops 16384 | bytes 65536 | tf_op jit(solution)/shard_map/psum | solution.py:160
  430.9 98.9 %all-gather.9.cloned.1.call-done = f32[8192,384]{1,0:T(8,128)} async-done(((f32[128,384]{1,0:T(8,128)}), f32[8192,384]{1,0:T(8,128)}) %all-gather.9.cloned.1.call-update) | async-done | bytes 12582928 | tf_op jit(solution)/shard_map/all_gather | solution.py:171
  529.8 5.3 reduce_sum.59
  (413 shorter events, 206.6 us)
Async XLA Ops:
  6.5 2.7 copy-start
  6.5 4.8 copy-start.14
  6.5 158.4 %all-gather.7.cloned.1.call-start = ((), (), s32[]{:S(2)}) async-start(), calls=%async_computation | async-start | bytes 25559040 | tf_op jit(solution)/shard_map/all_gather | solution.py:18
  9.3 2.8 copy-start.6
  9.3 3.3 copy-start.7
  16.0 1.3 copy-start.4
  17.2 512.6 %all-gather.9.cloned.1.call-start = ((), (), s32[]{:S(2)}) async-start(), calls=%async_computation.1 | async-start | bytes 12779520 | tf_op jit(solution)/shard_map/all_gather | solution.py:171
  80.5 2.7 copy-start.2
  152.9 2.7 copy-start.3
  155.7 8.7 %copy-start.11 = (s32[128,8]{0,1:T(8,128)S(1)}, s32[128,8]{0,1:T(8,128)}, u32[]{:S(2)}) copy-start(s32[128,8]{0,1:T(8,128)} %param.29) | copy-start | bytes 12292
  365.0 11.5 %copy-start.5 = (bf16[1536,384]{1,0:T(8,128)(2,1)S(1)}, bf16[1536,384]{1,0:T(8,128)(2,1)}, u32[]{:S(2)}) copy-start(bf16[1536,384]{1,0:T(8,128)(2,1)} %param.20) | copy-start | bytes 3538948
  365.0 19.4 %copy-start.8 = (bf16[40,384,8]{1,2,0:T(8,128)(2,1)S(1)}, bf16[40,384,8]{1,2,0:T(8,128)(2,1)}, u32[]{:S(2)}) copy-start(bf16[40,384,8]{1,2,0:T(8,128)(2,1)} %param.24) | copy-start | bytes 737284
  365.0 19.3 %copy-start.13 = (f32[384]{0:T(512)S(1)}, f32[384]{0:T(512)}, u32[]{:S(2)}) copy-start(f32[384]{0:T(512)} %param.21) | copy-start | bytes 4612
  384.7 6.7 %copy-start.9 = (bf16[40,384,8]{1,2,0:T(8,128)(2,1)S(1)}, bf16[40,384,8]{1,2,0:T(8,128)(2,1)}, u32[]{:S(2)}) copy-start(bf16[40,384,8]{1,2,0:T(8,128)(2,1)} %param.23) | copy-start | bytes 737284
  391.7 6.7 %copy-start.12 = (bf16[384,40]{0,1:T(8,128)(2,1)S(1)}, bf16[384,40]{0,1:T(8,128)(2,1)}, u32[]{:S(2)}) copy-start(bf16[384,40]{0,1:T(8,128)(2,1)} %param.22) | copy-start | bytes 92164
  416.7 13.2 %copy-start.10 = (bf16[40,8,384]{2,1,0:T(8,128)(2,1)S(1)}, bf16[40,8,384]{2,1,0:T(8,128)(2,1)}, u32[]{:S(2)}) copy-start(bf16[40,8,384]{2,1,0:T(8,128)(2,1)} %param.25) | copy-start | bytes 737284
  529.8 6.0 %copy-start.1 = (bf16[1536,640]{1,0:T(8,128)(2,1)S(1)}, bf16[1536,640]{1,0:T(8,128)(2,1)}, u32[]{:S(2)}) copy-start(bf16[1536,640]{1,0:T(8,128)(2,1)} %param.19) | copy-start | bytes 5898244
Sparse Core Ops, SparseCore 0:
  17.3 145.6 all-gather.6
  431.0 98.7 all-gather.8
